TPU v7x, 32 devices: a whole 2x2x4 slice. The times are simulated.
32 devices in a mesh: parts: 2 (over y), users: 16 (over z, x, core).
Axes of the slice: x: 2, y: 2, z: 4, core: 2. Of those that a mesh axis runs over, the one named last changes fastest.
Arguments:
- candidates: bfloat16 [512, 512], P(('parts', 'users')), parts along dimension 0, may hold values from -6 to 6
- candidate_user: int32 [512], P(('parts', 'users')), parts along dimension 0, may hold values from 0 to 7
- events: bfloat16 [65536, 512], P(('parts', 'users')), parts along dimension 0, may hold values from -6 to 6
- event_user: int32 [65536], P(('parts', 'users')), parts along dimension 0, may hold values from 0 to 7, never falling along the last dimension, each value on 1 to 12288 neighbouring positions
- event_mask: int32 [65536], P(('parts', 'users')), parts along dimension 0, may hold values 0 or 1
- query_weight: bfloat16 [512, 512], replicated, may hold values from -0.25 to 0.25
- key_weight: bfloat16 [512, 512], replicated, may hold values from -0.25 to 0.25
- value_weight: bfloat16 [512, 512], replicated, may hold values from -2 to 2
- gate_weight: bfloat16 [512, 512], replicated, may hold values from -0.25 to 0.25
- output_weight: bfloat16 [512, 512], replicated, may hold values from -0.25 to 0.25
Outputs:
- candidate_out: bfloat16 [512, 512], P(('parts', 'users')), parts along dimension 0
There are 2 independent parts, one for each index of `parts`. A program takes and returns all parts, laid end to end along the dimension named above; an argument that names none is the same for every part. Nothing has to cross between parts.
Inputs may be any that keep to these rules, and one draw needn't show every extreme that they name: event_user never falls along the events; each user's events form one run of at most 12288 slots.
All inputs are finite; a program needn't handle non-finite values. No bound on the sum of `event_mask` on one device may be relied on, other than what follows from the above.
Results may differ from a plain program's by a relative error of at most 0.0044.
Values may be sent and summed in bfloat16 or wider, within the bound.
No kernel may reach another device: no remote copies, remote signals or barrier semaphores. Data moves between devices by JAX's collectives and lax.ppermute only.
A program may use at most 64 MiB of HBM per device.

v0:
```python
import math
import jax
import jax.numpy as jnp
from jax import lax
from jax.sharding import PartitionSpec as P

HEADS = 4


def per_device(
    candidates,
    candidate_user,
    events,
    event_user,
    event_mask,
    query_weight,
    key_weight,
    value_weight,
    gate_weight,
    output_weight,
):
    own_count = candidates.shape[0]
    model_width = candidates.shape[1]
    head_count = HEADS
    head_size = model_width // head_count
    score_scale = 1.0 / math.sqrt(head_size)
    queries = jnp.dot(candidates, query_weight, preferred_element_type=jnp.float32).astype(
        jnp.bfloat16
    )
    gate_values = jax.nn.silu(jnp.dot(candidates, gate_weight, preferred_element_type=jnp.float32))
    key_rows = jnp.dot(events, key_weight, preferred_element_type=jnp.float32).astype(jnp.bfloat16)
    value_rows = jnp.dot(events, value_weight, preferred_element_type=jnp.float32).astype(
        jnp.bfloat16
    )
    event_count = key_rows.shape[0]
    key_heads = key_rows.reshape(event_count, head_count, head_size)
    value_heads = value_rows.reshape(event_count, head_count, head_size)
    valid_events = event_mask.astype(jnp.float32)
    all_queries, all_users = (
        lax.all_gather(queries, "users", axis=0, tiled=True),
        lax.all_gather(candidate_user, "users", axis=0, tiled=True),
    )

    def one_block(block_pair):
        query_block, user_block = block_pair
        scores = (
            jnp.einsum("chd,ehd->hce", query_block, key_heads, preferred_element_type=jnp.float32)
            * score_scale
        )
        same_user = (user_block[:, None] == event_user[None, :]).astype(jnp.float32) * valid_events[
            None, :
        ]
        attn_weights = (jax.nn.silu(scores) * same_user[None]).astype(jnp.bfloat16)
        mixed_rows = jnp.einsum(
            "hce,ehd->chd", attn_weights, value_heads, preferred_element_type=jnp.float32
        )
        return mixed_rows.reshape(query_block.shape[0], model_width)

    row_count = own_count * lax.axis_size("users")
    row_block = math.gcd(row_count, 512)
    query_part = all_queries
    query_part = query_part.reshape(row_count // row_block, row_block, head_count, head_size)
    user_part = all_users.reshape(row_count // row_block, row_block)
    summed = lax.psum_scatter(
        lax.map(one_block, (query_part, user_part)).reshape(row_count, model_width),
        "users",
        scatter_dimension=0,
        tiled=True,
    )
    mean_row = jnp.mean(summed, axis=1, keepdims=True)
    centred = summed - mean_row
    var_row = jnp.mean(centred * centred, axis=1, keepdims=True)
    normed = centred / jnp.sqrt(var_row + 1e-05)
    gated_rows = (normed * gate_values).astype(jnp.bfloat16)
    result = candidates.astype(jnp.float32) + jnp.dot(
        gated_rows, output_weight, preferred_element_type=jnp.float32
    )
    return result.astype(jnp.bfloat16)


def solution(mesh):
    in_specs = (
        P(("parts", "users"), None),
        P(("parts", "users")),
        P(("parts", "users"), None),
        P(("parts", "users")),
        P(("parts", "users")),
        P(),
        P(),
        P(),
        P(),
        P(),
    )
    out_specs = P(("parts", "users"), None)
    return jax.shard_map(
        per_device, mesh=mesh, in_specs=in_specs, out_specs=out_specs, check_vma=False
    )
```

profile of v0, /device:TPU:0, one launch (start us, length us, event | category | flops | bytes accessed | tf_op | source)
XLA Modules:
  0.0 126.6 jit_solution(15532757817765731174)
XLA Ops:
  6.5 0.0 copy-start
  6.5 0.0 reduce-scatter.2.cloned.1.call-start
  6.5 1.4 %dynamic-slice.1 = u32[1]{0:T(128)} dynamic-slice(u32[32]{0:T(128)} %constant.34, u32[]{:T(128)S(6)} %add.28), dynamic_slice_sizes={1} | dynamic-slice | bytes 12
  8.6 0.9 dynamic-update-slice
  9.4 13.7 %all-reduce = s32[256]{0:T(256)S(1)} all-reduce(s32[256]{0:T(256)S(1)} %dynamic-update-slice), channel_id=1, replica_groups=mesh['parts'=2,'users'=16] {'users'}, use_global_device_ids=true, to_apply=%add | all-reduce | flops 256 | bytes 2048
  23.2 0.7 convert_element_type.31
  23.9 1.2 convolution_convert_fusion.2
  25.1 18.7 %all_gather.6 = bf16[256,512]{1,0:T(8,128)(2,1)S(1)} all-gather(bf16[16,512]{1,0:T(8,128)(2,1)S(1)} %convolution_convert_fusion.2), channel_id=1, replica_groups=mesh['parts'=2,'users'=16] {'users'}, dimensions={0}, use_global_device_ids=true | all-gather | bytes 278528 | tf_op jit(solution)/shard_map/all_gather | solution.py:40
  43.8 0.0 copy-done
  43.8 0.0 copy-start.5
  43.8 3.7 %convolution_convert_fusion = bf16[2048,512]{0,1:T(8,128)(2,1)} fusion(bf16[2048,512]{1,0:T(8,128)(2,1)S(1)} %copy-done, bf16[512,512]{1,0:T(8,128)(2,1)} %param.16), kind=kOutput, calls=%fused_computation.1 | convolution fusion | flops 1074790400 | bytes 4718592 | tf_op jit(solution)/shard_map/dot_general | solution.py:31
  47.5 0.0 copy-done.5
  47.5 0.0 copy-start.4
  47.5 2.7 %convolution_convert_fusion.1 = bf16[2048,512]{0,1:T(8,128)(2,1)} fusion(bf16[2048,512]{1,0:T(8,128)(2,1)S(1)} %copy-done, bf16[512,512]{1,0:T(8,128)(2,1)S(1)} %copy-done.5), kind=kOutput, calls=%fused_computation.2 | convolution fusion | flops 1074790400 | bytes 4718592 | tf_op jit(solution)/shard_map/dot_general | solution.py:32
  50.1 0.0 copy-done.4
  50.1 1.5 %compare_select_fusion = f32[256,2048]{1,0:T(8,128)} fusion(f32[2048]{0:T(1024)S(1)} %convert_element_type.31, s32[2048]{0:T(1024)S(1)} %copy-done.4, s32[256]{0:T(256)S(1)} %all-reduce), kind=kLoop, calls=%fused_computation.3 | loop fusion | flops 1048576 | bytes 2114560 | tf_op jit(solution)/shard_map/while/body/eval_jaxpr/mul | solution.py:50
  51.7 0.0 copy-start.1
  51.7 0.0 copy-start.2
  51.7 0.0 copy-start.3
  51.7 8.2 %fusion = f32[4,128,256]{2,1,0:T(8,128)} fusion(bf16[2048,4,128]{0,2,1:T(8,128)(2,1)} %bitcast.28, bf16[2048,4,128]{0,2,1:T(8,128)(2,1)} %bitcast.27, f32[256,2048]{1,0:T(8,128)} %compare_select_fusion, bf16[256,512]{1,0:T(8,128)(2,1)S(1)} %all_gather.6), kind=kOutput, calls=%fused_computation.4 | convolution fusion | flops 1088421888 | bytes 7077888 | tf_op jit(solution)/shard_map/while/body/eval_jaxpr/hce,ehd->chd/dot_general | solution.py:54
  59.9 2.0 %copy.13 = f32[256,512]{1,0:T(8,128)} copy(f32[256,512]{0,1:T(8,128)} %bitcast.26) | data formatting | bytes 1048576 | tf_op jit(solution)/shard_map/reshape | solution.py:65
  61.9 0.0 reduce-scatter.2.cloned.1.call-update
  61.9 54.3 %reduce-scatter.2.cloned.1.call-done = f32[16,512]{1,0:T(8,128)} async-done(((f32[256,512]{1,0:T(8,128)}), f32[16,512]{1,0:T(8,128)}) %reduce-scatter.2.cloned.1.call-update) | async-done | bytes 32784 | tf_op jit(solution)/shard_map/reduce_scatter | solution.py:64
  116.2 0.9 reduce_sum.18
  117.1 0.9 multiply_reduce_fusion
  118.0 0.0 copy-done.1
  118.0 0.0 copy-done.2
  118.1 0.0 copy-done.3
  118.1 1.7 %fusion.1 = bf16[16,512]{1,0:T(8,128)(2,1)} fusion(bf16[512,512]{1,0:T(8,128)(2,1)S(1)} %copy-done.1, bf16[16,512]{1,0:T(8,128)(2,1)S(1)} %copy-done.3, f32[16,512]{1,0:T(8,128)} %reduce-scatter.2.cloned.1.call-done, f32[16]{0:T(128)S(1)} %add_sqrt_fusion, f32[16]{0:T(128)S(1)} %broadcast_multiply_fusion, bf16[512,512]{1,0:T(8,128)(2,1)S(1)} %copy-done.2), kind=kOutput, calls=%fused_computation.6 | convolution fusion | flops 16867328 | bytes 1114240 | tf_op jit(solution)/shard_map/dot_general | solution.py:75
  (3 shorter events, 0.0 us)
Async XLA Ops:
  6.5 37.2 %copy-start = (bf16[2048,512]{1,0:T(8,128)(2,1)S(1)}, bf16[2048,512]{1,0:T(8,128)(2,1)}, u32[]{:S(2)}) copy-start(bf16[2048,512]{1,0:T(8,128)(2,1)} %param.12) | copy-start | bytes 6291460
  6.5 109.7 %reduce-scatter.2.cloned.1.call-start = ((), (), s32[]{:S(2)}) async-start(), calls=%async_computation.1 | async-start | bytes 557056 | tf_op jit(solution)/shard_map/reduce_scatter | solution.py:64
  43.8 3.7 %copy-start.5 = (bf16[512,512]{1,0:T(8,128)(2,1)S(1)}, bf16[512,512]{1,0:T(8,128)(2,1)}, u32[]{:S(2)}) copy-start(bf16[512,512]{1,0:T(8,128)(2,1)} %param.17) | copy-start | bytes 1572868
  47.5 2.7 %copy-start.4 = (s32[2048]{0:T(1024)S(1)}, s32[2048]{0:T(1024)}, u32[]{:S(2)}) copy-start(s32[2048]{0:T(1024)} %param.13) | copy-start | bytes 24580
  51.7 66.4 %copy-start.1 = (bf16[512,512]{1,0:T(8,128)(2,1)S(1)}, bf16[512,512]{1,0:T(8,128)(2,1)}, u32[]{:S(2)}) copy-start(bf16[512,512]{1,0:T(8,128)(2,1)} %param.19) | copy-start | bytes 1572868
  51.7 66.4 %copy-start.2 = (bf16[512,512]{1,0:T(8,128)(2,1)S(1)}, bf16[512,512]{1,0:T(8,128)(2,1)}, u32[]{:S(2)}) copy-start(bf16[512,512]{1,0:T(8,128)(2,1)} %param.18) | copy-start | bytes 1572868
  51.7 66.4 %copy-start.3 = (bf16[16,512]{1,0:T(8,128)(2,1)S(1)}, bf16[16,512]{1,0:T(8,128)(2,1)}, u32[]{:S(2)}) copy-start(bf16[16,512]{1,0:T(8,128)(2,1)} %param.10) | copy-start | bytes 49156
Sparse Core Ops, SparseCore 0:
  62.0 54.1 reduce-scatter.1
where the time goes:
time: 127 us
  waiting for transfers between devices  54.3 us (43%)
  blocking collectives  32.4 us (26%)
  matrix products  17.5 us (14%)
  between operations  14.1 us (11%)
  local copies, waits for them, and re-layouts  4.3 us (3%)
  other arithmetic  4.07 us (3%)
    reduce_scatter x1, waiting for transfers between devices, per_device(): lax.psum_scatter(lax.map(one_block, (query_part, user_part)).reshape(row_...  54.3 us
    all_gather x1, blocking collectives, per_device(): lax.all_gather(queries, 'users', axis=0, tiled=True)  18.7 us
    unnamed x1, blocking collectives  13.7 us
    dot_general x1, matrix products, one_block(): jnp.einsum('hce,ehd->chd', attn_weights, value_heads, preferred_element_t...  8.19 us
    dot_general x1, matrix products, per_device(): jnp.dot(events, key_weight, preferred_element_type=jnp.float32)  3.69 us
    dot_general x1, matrix products, per_device(): jnp.dot(events, value_weight, preferred_element_type=jnp.float32)  2.65 us
  transfers between devices with their start and end apart: 1, of which 1 were waited for; matrix products, arithmetic and copies ran while one was open for 0% of the time, Pallas kernels for 0%

commit v1 on v0

--- a/solution.py
+++ b/solution.py
@@ -5,6 +5,19 @@
 from jax.sharding import PartitionSpec as P
 
 HEADS = 4
+
+
+def gather_around(shard, axis, dim):
+    ways = lax.axis_size(axis)
+    up = [(d, (d + 1) % ways) for d in range(ways)]
+    down = [(d, (d - 1) % ways) for d in range(ways)]
+    earlier, later = ([shard], [shard])
+    for _ in range(ways // 2):
+        earlier.append(lax.ppermute(earlier[-1], axis, up))
+    for _ in range((ways - 1) // 2):
+        later.append(lax.ppermute(later[-1], axis, down))
+    line = jnp.concatenate([*earlier[::-1], *later[1:]], axis=dim)
+    return jnp.roll(line, (lax.axis_index(axis) - ways // 2) * shard.shape[dim], axis=dim)
 
 
 def per_device(
@@ -37,7 +50,7 @@
     value_heads = value_rows.reshape(event_count, head_count, head_size)
     valid_events = event_mask.astype(jnp.float32)
     all_queries, all_users = (
-        lax.all_gather(queries, "users", axis=0, tiled=True),
+        gather_around(queries, "users", 0),
         lax.all_gather(candidate_user, "users", axis=0, tiled=True),
     )
 

time: 127 us -> 150 us (1.18)
  starting transfers between devices: 0.01 us -> 27.2 us
  blocking collectives: 32.4 us -> 12.1 us
  waiting for transfers between devices: 54.3 us -> 69.9 us
    ppermute x0 -> x15, starting transfers between devices: none -> 27.2 us  [the longest x7 26.2 us: gather_around(): later.append(lax.ppermute(later[-1], axis, down))]
    all_gather x1 -> x0, blocking collectives: 18.7 us -> none  [per_device(): lax.all_gather(queries, 'users', axis=0, tiled=True)]
    ppermute x0 -> x15, waiting for transfers between devices: none -> 12 us  [the longest x8 10.6 us: gather_around(): earlier.append(lax.ppermute(earlier[-1], axis, up))]
    reduce_scatter x1, waiting for transfers between devices: 54.3 us -> 58 us  [per_device(): lax.psum_scatter(lax.map(one_block, (query_part, user_part)).reshape(row_...]
    unnamed x1, blocking collectives: 13.7 us -> 12.1 us
  transfers between devices with their start and end apart: 1 -> 16, of which waited for: 1 -> 6; matrix products, arithmetic and copies ran while one was open for 0% -> 7% of each run, Pallas kernels for 0% -> 0%
where the time goes in v1:
time: 150 us; the launch traced here: 149 us
  waiting for transfers between devices  69.9 us (47%)
  starting transfers between devices  27.2 us (18%)
  matrix products  16.5 us (11%)
  between operations  14.4 us (10%)
  blocking collectives  12.1 us (8%)
  other arithmetic  4.76 us (3%)
  local copies, waits for them, and re-layouts  4.44 us (3%)
    reduce_scatter x1, waiting for transfers between devices, per_device(): lax.psum_scatter(lax.map(one_block, (query_part, user_part)).reshape(row_...  58 us
    ppermute x7, starting transfers between devices, gather_around(): later.append(lax.ppermute(later[-1], axis, down))  26.2 us
    unnamed x1, blocking collectives  12.1 us
    ppermute x8, waiting for transfers between devices, gather_around(): earlier.append(lax.ppermute(earlier[-1], axis, up))  10.6 us
    dot_general x1, matrix products, one_block(): jnp.einsum('hce,ehd->chd', attn_weights, value_heads, preferred_element_t...  8.14 us
  transfers between devices with their start and end apart: 16, of which 6 were waited for; matrix products, arithmetic and copies ran while one was open for 7% of the time, Pallas kernels for 0%

profile of v1, /device:TPU:0, one launch (start us, length us, event | category | flops | bytes accessed | tf_op | source)
XLA Modules:
  0.0 149.2 jit_solution(16934273846662759990)
XLA Ops:
  6.5 1.4 convolution_convert_fusion.2
  7.9 0.5 collective-permute-start
  8.4 6.4 %collective-permute-done = bf16[16,512]{1,0:T(8,128)(2,1)S(1)} collective-permute-done((bf16[16,512]{1,0:T(8,128)(2,1)S(1)}, bf16[16,512]{1,0:T(8,128)(2,1)S(1)}, u32[]{:S(2)}, u32[]{:S(2)}) %collective-permute-start) | collective-permute-done | bytes 16416 | tf_op jit(solution)/shard_map/ppermute | solution.py:16
  14.8 4.4 %collective-permute-start.8 = (bf16[16,512]{1,0:T(8,128)(2,1)S(1)}, bf16[16,512]{1,0:T(8,128)(2,1)S(1)}, u32[]{:S(2)}, u32[]{:S(2)}) collective-permute-start(bf16[16,512]{1,0:T(8,128)(2,1)S(1)} %convolution_convert_fusion.2), channel_id=1, source_target_pairs={{0,15},{1,0},{2,1},{3,2},{4,3},{5,4},{6,5},{7,6},{8,7},{9,8},{10,9... | collective-permute-start | bytes 49160 | tf_op jit(solution)/shard_map/ppermute | solution.py:18
  19.2 1.4 collective-permute-done.1
  20.7 0.0 collective-permute-done.8
  20.7 4.4 %collective-permute-start.9 = (bf16[16,512]{1,0:T(8,128)(2,1)S(1)}, bf16[16,512]{1,0:T(8,128)(2,1)S(1)}, u32[]{:S(2)}, u32[]{:S(2)}) collective-permute-start(bf16[16,512]{1,0:T(8,128)(2,1)S(1)} %collective-permute-done.8), channel_id=1, source_target_pairs={{0,15},{1,0},{2,1},{3,2},{4,3},{5,4},{6,5},{7,6},{8,7},{9,8},{10,9... | collective-permute-start | bytes 49160 | tf_op jit(solution)/shard_map/ppermute | solution.py:18
  25.1 1.4 collective-permute-done.2
  26.5 0.0 collective-permute-done.9
  26.5 4.4 %collective-permute-start.10 = (bf16[16,512]{1,0:T(8,128)(2,1)S(1)}, bf16[16,512]{1,0:T(8,128)(2,1)S(1)}, u32[]{:S(2)}, u32[]{:S(2)}) collective-permute-start(bf16[16,512]{1,0:T(8,128)(2,1)S(1)} %collective-permute-done.9), channel_id=1, source_target_pairs={{0,15},{1,0},{2,1},{3,2},{4,3},{5,4},{6,5},{7,6},{8,7},{9,8},{10,9... | collective-permute-start | bytes 49160 | tf_op jit(solution)/shard_map/ppermute | solution.py:18
  31.0 1.4 collective-permute-done.3
  32.4 0.7 convert_element_type.31
  33.1 1.2 dynamic-slice.1
  35.0 0.9 dynamic-update-slice
  35.8 12.1 %all-reduce = s32[256]{0:T(256)S(1)} all-reduce(s32[256]{0:T(256)S(1)} %dynamic-update-slice), channel_id=1, replica_groups=mesh['parts'=2,'users'=16] {'users'}, use_global_device_ids=true, to_apply=%add | all-reduce | flops 256 | bytes 2048
  47.9 0.5 collective-permute-start.5
  48.4 2.2 %compare_select_fusion = f32[256,2048]{1,0:T(8,128)} fusion(f32[2048]{0:T(1024)S(1)} %convert_element_type.31, s32[2048]{0:T(1024)} %param.13, s32[256]{0:T(256)S(1)} %all-reduce), kind=kLoop, calls=%fused_computation.3 | loop fusion | flops 1048576 | bytes 2114560 | tf_op jit(solution)/shard_map/while/body/eval_jaxpr/mul | solution.py:63
  50.7 4.0 %collective-permute-start.12 = (bf16[16,512]{1,0:T(8,128)(2,1)S(1)}, bf16[16,512]{1,0:T(8,128)(2,1)S(1)}, u32[]{:S(2)}, u32[]{:S(2)}) collective-permute-start(bf16[16,512]{1,0:T(8,128)(2,1)S(1)} %collective-permute-done.11), channel_id=1, source_target_pairs={{0,15},{1,0},{2,1},{3,2},{4,3},{5,4},{6,5},{7,6},{8,7},{9,8},{10,9... | collective-permute-start | bytes 49160 | tf_op jit(solution)/shard_map/ppermute | solution.py:18
  54.7 2.6 %convolution_convert_fusion = bf16[2048,512]{0,1:T(8,128)(2,1)} fusion(bf16[2048,512]{1,0:T(8,128)(2,1)S(1)} %copy-done, bf16[512,512]{1,0:T(8,128)(2,1)S(1)} %copy-done.4), kind=kOutput, calls=%fused_computation.1 | convolution fusion | flops 1074790400 | bytes 4718592 | tf_op jit(solution)/shard_map/dot_general | solution.py:44
  57.3 4.4 %collective-permute-start.13 = (bf16[16,512]{1,0:T(8,128)(2,1)S(1)}, bf16[16,512]{1,0:T(8,128)(2,1)S(1)}, u32[]{:S(2)}, u32[]{:S(2)}) collective-permute-start(bf16[16,512]{1,0:T(8,128)(2,1)S(1)} %collective-permute-done.12), channel_id=1, source_target_pairs={{0,15},{1,0},{2,1},{3,2},{4,3},{5,4},{6,5},{7,6},{8,7},{9,8},{10,9... | collective-permute-start | bytes 49160 | tf_op jit(solution)/shard_map/ppermute | solution.py:18
  61.7 2.6 %convolution_convert_fusion.1 = bf16[2048,512]{0,1:T(8,128)(2,1)} fusion(bf16[2048,512]{1,0:T(8,128)(2,1)S(1)} %copy-done, bf16[512,512]{1,0:T(8,128)(2,1)S(1)} %copy-done.5), kind=kOutput, calls=%fused_computation.2 | convolution fusion | flops 1074790400 | bytes 4718592 | tf_op jit(solution)/shard_map/dot_general | solution.py:45
  64.4 4.4 %collective-permute-start.14 = (bf16[16,512]{1,0:T(8,128)(2,1)S(1)}, bf16[16,512]{1,0:T(8,128)(2,1)S(1)}, u32[]{:S(2)}, u32[]{:S(2)}) collective-permute-start(bf16[16,512]{1,0:T(8,128)(2,1)S(1)} %collective-permute-done.13), channel_id=1, source_target_pairs={{0,15},{1,0},{2,1},{3,2},{4,3},{5,4},{6,5},{7,6},{8,7},{9,8},{10,9... | collective-permute-start | bytes 49160 | tf_op jit(solution)/shard_map/ppermute | solution.py:18
  69.0 1.3 collective-permute-done.14
  70.5 0.1 copy.13
  70.6 0.0 copy-start.1
  70.6 8.1 %fusion = f32[4,128,256]{2,1,0:T(8,128)} fusion(bf16[2048,4,128]{0,2,1:T(8,128)(2,1)} %bitcast.22, bf16[256,4,128]{0,2,1:T(8,128)(2,1)S(1)} %bitcast.20, bf16[2048,4,128]{0,2,1:T(8,128)(2,1)} %bitcast.21, f32[256,2048]{1,0:T(8,128)} %compare_select_fusion), kind=kOutput, calls=%fused_computation.4 | convolution fusion | flops 1088421888 | bytes 7077888 | tf_op jit(solution)/shard_map/while/body/eval_jaxpr/hce,ehd->chd/dot_general | solution.py:67
  78.8 2.0 %copy.16 = f32[256,512]{1,0:T(8,128)} copy(f32[256,512]{0,1:T(8,128)} %bitcast.19) | data formatting | bytes 1048576 | tf_op jit(solution)/shard_map/reshape | solution.py:78
  80.8 0.0 reduce-scatter.2.cloned.1.call-update
  80.9 58.0 %reduce-scatter.2.cloned.1.call-done = f32[16,512]{1,0:T(8,128)} async-done(((f32[256,512]{1,0:T(8,128)}), f32[16,512]{1,0:T(8,128)}) %reduce-scatter.2.cloned.1.call-update) | async-done | bytes 32784 | tf_op jit(solution)/shard_map/reduce_scatter | solution.py:77
  138.8 0.9 reduce_sum.18
  139.7 0.9 multiply_reduce_fusion
  140.7 1.7 %fusion.1 = bf16[16,512]{1,0:T(8,128)(2,1)} fusion(bf16[512,512]{1,0:T(8,128)(2,1)S(1)} %copy-done.1, bf16[16,512]{1,0:T(8,128)(2,1)S(1)} %copy-done.3, f32[16,512]{1,0:T(8,128)} %reduce-scatter.2.cloned.1.call-done, f32[16]{0:T(128)S(1)} %add_sqrt_fusion, f32[16]{0:T(128)S(1)} %broadcast_multiply_fusion, bf16[512,512]{1,0:T(8,128)(2,1)S(1)} %copy-done.2), kind=kOutput, calls=%fused_computation.6 | convolution fusion | flops 16867328 | bytes 1114240 | tf_op jit(solution)/shard_map/dot_general | solution.py:88
  (63 shorter events, 0.2 us)
Async XLA Ops:
  6.5 48.1 %copy-start = (bf16[2048,512]{1,0:T(8,128)(2,1)S(1)}, bf16[2048,512]{1,0:T(8,128)(2,1)}, u32[]{:S(2)}) copy-start(bf16[2048,512]{1,0:T(8,128)(2,1)} %param.12) | copy-start | bytes 6291460
  6.5 48.1 %copy-start.4 = (bf16[512,512]{1,0:T(8,128)(2,1)S(1)}, bf16[512,512]{1,0:T(8,128)(2,1)}, u32[]{:S(2)}) copy-start(bf16[512,512]{1,0:T(8,128)(2,1)} %param.16) | copy-start | bytes 1572868
  6.5 132.3 %reduce-scatter.2.cloned.1.call-start = ((), (), s32[]{:S(2)}) async-start(), calls=%async_computation.1 | async-start | bytes 557056 | tf_op jit(solution)/shard_map/reduce_scatter | solution.py:77
  7.9 6.9 %collective-permute-start = (bf16[16,512]{1,0:T(8,128)(2,1)S(1)}, bf16[16,512]{1,0:T(8,128)(2,1)S(1)}, u32[]{:S(2)}, u32[]{:S(2)}) collective-permute-start(bf16[16,512]{1,0:T(8,128)(2,1)S(1)} %convolution_convert_fusion.2), channel_id=1, source_target_pairs={{0,1},{1,2},{2,3},{3,4},{4,5},{5,6},{6,7},{7,8},{8,9},{9,10},{10,1... | collective-permute-start | bytes 49160 | tf_op jit(solution)/shard_map/ppermute | solution.py:16
  14.8 5.9 %collective-permute-start.1 = (bf16[16,512]{1,0:T(8,128)(2,1)S(1)}, bf16[16,512]{1,0:T(8,128)(2,1)S(1)}, u32[]{:S(2)}, u32[]{:S(2)}) collective-permute-start(bf16[16,512]{1,0:T(8,128)(2,1)S(1)} %collective-permute-done), channel_id=1, source_target_pairs={{0,1},{1,2},{2,3},{3,4},{4,5},{5,6},{6,7},{7,8},{8,9},{9,10},{10,1... | collective-permute-start | bytes 49160 | tf_op jit(solution)/shard_map/ppermute | solution.py:16
  14.8 5.9 %collective-permute-start.8 = (bf16[16,512]{1,0:T(8,128)(2,1)S(1)}, bf16[16,512]{1,0:T(8,128)(2,1)S(1)}, u32[]{:S(2)}, u32[]{:S(2)}) collective-permute-start(bf16[16,512]{1,0:T(8,128)(2,1)S(1)} %convolution_convert_fusion.2), channel_id=1, source_target_pairs={{0,15},{1,0},{2,1},{3,2},{4,3},{5,4},{6,5},{7,6},{8,7},{9,8},{10,9... | collective-permute-start | bytes 49160 | tf_op jit(solution)/shard_map/ppermute | solution.py:18
  20.7 5.9 %collective-permute-start.2 = (bf16[16,512]{1,0:T(8,128)(2,1)S(1)}, bf16[16,512]{1,0:T(8,128)(2,1)S(1)}, u32[]{:S(2)}, u32[]{:S(2)}) collective-permute-start(bf16[16,512]{1,0:T(8,128)(2,1)S(1)} %collective-permute-done.1), channel_id=1, source_target_pairs={{0,1},{1,2},{2,3},{3,4},{4,5},{5,6},{6,7},{7,8},{8,9},{9,10},{10,1... | collective-permute-start | bytes 49160 | tf_op jit(solution)/shard_map/ppermute | solution.py:16
  20.7 5.9 %collective-permute-start.9 = (bf16[16,512]{1,0:T(8,128)(2,1)S(1)}, bf16[16,512]{1,0:T(8,128)(2,1)S(1)}, u32[]{:S(2)}, u32[]{:S(2)}) collective-permute-start(bf16[16,512]{1,0:T(8,128)(2,1)S(1)} %collective-permute-done.8), channel_id=1, source_target_pairs={{0,15},{1,0},{2,1},{3,2},{4,3},{5,4},{6,5},{7,6},{8,7},{9,8},{10,9... | collective-permute-start | bytes 49160 | tf_op jit(solution)/shard_map/ppermute | solution.py:18
  26.5 5.9 %collective-permute-start.3 = (bf16[16,512]{1,0:T(8,128)(2,1)S(1)}, bf16[16,512]{1,0:T(8,128)(2,1)S(1)}, u32[]{:S(2)}, u32[]{:S(2)}) collective-permute-start(bf16[16,512]{1,0:T(8,128)(2,1)S(1)} %collective-permute-done.2), channel_id=1, source_target_pairs={{0,1},{1,2},{2,3},{3,4},{4,5},{5,6},{6,7},{7,8},{8,9},{9,10},{10,1... | collective-permute-start | bytes 49160 | tf_op jit(solution)/shard_map/ppermute | solution.py:16
  26.5 21.4 %collective-permute-start.10 = (bf16[16,512]{1,0:T(8,128)(2,1)S(1)}, bf16[16,512]{1,0:T(8,128)(2,1)S(1)}, u32[]{:S(2)}, u32[]{:S(2)}) collective-permute-start(bf16[16,512]{1,0:T(8,128)(2,1)S(1)} %collective-permute-done.9), channel_id=1, source_target_pairs={{0,15},{1,0},{2,1},{3,2},{4,3},{5,4},{6,5},{7,6},{8,7},{9,8},{10,9... | collective-permute-start | bytes 49160 | tf_op jit(solution)/shard_map/ppermute | solution.py:18
  32.4 15.5 %collective-permute-start.4 = (bf16[16,512]{1,0:T(8,128)(2,1)S(1)}, bf16[16,512]{1,0:T(8,128)(2,1)S(1)}, u32[]{:S(2)}, u32[]{:S(2)}) collective-permute-start(bf16[16,512]{1,0:T(8,128)(2,1)S(1)} %collective-permute-done.3), channel_id=1, source_target_pairs={{0,1},{1,2},{2,3},{3,4},{4,5},{5,6},{6,7},{7,8},{8,9},{9,10},{10,1... | collective-permute-start | bytes 49160 | tf_op jit(solution)/shard_map/ppermute | solution.py:16
  47.9 2.7 %collective-permute-start.11 = (bf16[16,512]{1,0:T(8,128)(2,1)S(1)}, bf16[16,512]{1,0:T(8,128)(2,1)S(1)}, u32[]{:S(2)}, u32[]{:S(2)}) collective-permute-start(bf16[16,512]{1,0:T(8,128)(2,1)S(1)} %collective-permute-done.10), channel_id=1, source_target_pairs={{0,15},{1,0},{2,1},{3,2},{4,3},{5,4},{6,5},{7,6},{8,7},{9,8},{10,9... | collective-permute-start | bytes 49160 | tf_op jit(solution)/shard_map/ppermute | solution.py:18
  47.9 6.7 %collective-permute-start.5 = (bf16[16,512]{1,0:T(8,128)(2,1)S(1)}, bf16[16,512]{1,0:T(8,128)(2,1)S(1)}, u32[]{:S(2)}, u32[]{:S(2)}) collective-permute-start(bf16[16,512]{1,0:T(8,128)(2,1)S(1)} %collective-permute-done.4), channel_id=1, source_target_pairs={{0,1},{1,2},{2,3},{3,4},{4,5},{5,6},{6,7},{7,8},{8,9},{9,10},{10,1... | collective-permute-start | bytes 49160 | tf_op jit(solution)/shard_map/ppermute | solution.py:16
  50.7 11.1 %copy-start.5 = (bf16[512,512]{1,0:T(8,128)(2,1)S(1)}, bf16[512,512]{1,0:T(8,128)(2,1)}, u32[]{:S(2)}) copy-start(bf16[512,512]{1,0:T(8,128)(2,1)} %param.17) | copy-start | bytes 1572868
  50.7 6.6 %collective-permute-start.12 = (bf16[16,512]{1,0:T(8,128)(2,1)S(1)}, bf16[16,512]{1,0:T(8,128)(2,1)S(1)}, u32[]{:S(2)}, u32[]{:S(2)}) collective-permute-start(bf16[16,512]{1,0:T(8,128)(2,1)S(1)} %collective-permute-done.11), channel_id=1, source_target_pairs={{0,15},{1,0},{2,1},{3,2},{4,3},{5,4},{6,5},{7,6},{8,7},{9,8},{10,9... | collective-permute-start | bytes 49160 | tf_op jit(solution)/shard_map/ppermute | solution.py:18
  54.7 7.1 %collective-permute-start.6 = (bf16[16,512]{1,0:T(8,128)(2,1)S(1)}, bf16[16,512]{1,0:T(8,128)(2,1)S(1)}, u32[]{:S(2)}, u32[]{:S(2)}) collective-permute-start(bf16[16,512]{1,0:T(8,128)(2,1)S(1)} %collective-permute-done.5), channel_id=1, source_target_pairs={{0,1},{1,2},{2,3},{3,4},{4,5},{5,6},{6,7},{7,8},{8,9},{9,10},{10,1... | collective-permute-start | bytes 49160 | tf_op jit(solution)/shard_map/ppermute | solution.py:16
  57.3 7.1 %collective-permute-start.13 = (bf16[16,512]{1,0:T(8,128)(2,1)S(1)}, bf16[16,512]{1,0:T(8,128)(2,1)S(1)}, u32[]{:S(2)}, u32[]{:S(2)}) collective-permute-start(bf16[16,512]{1,0:T(8,128)(2,1)S(1)} %collective-permute-done.12), channel_id=1, source_target_pairs={{0,15},{1,0},{2,1},{3,2},{4,3},{5,4},{6,5},{7,6},{8,7},{9,8},{10,9... | collective-permute-start | bytes 49160 | tf_op jit(solution)/shard_map/ppermute | solution.py:18
  61.7 7.1 %collective-permute-start.7 = (bf16[16,512]{1,0:T(8,128)(2,1)S(1)}, bf16[16,512]{1,0:T(8,128)(2,1)S(1)}, u32[]{:S(2)}, u32[]{:S(2)}) collective-permute-start(bf16[16,512]{1,0:T(8,128)(2,1)S(1)} %collective-permute-done.6), channel_id=1, source_target_pairs={{0,1},{1,2},{2,3},{3,4},{4,5},{5,6},{6,7},{7,8},{8,9},{9,10},{10,1... | collective-permute-start | bytes 49160 | tf_op jit(solution)/shard_map/ppermute | solution.py:16
  64.4 5.9 %collective-permute-start.14 = (bf16[16,512]{1,0:T(8,128)(2,1)S(1)}, bf16[16,512]{1,0:T(8,128)(2,1)S(1)}, u32[]{:S(2)}, u32[]{:S(2)}) collective-permute-start(bf16[16,512]{1,0:T(8,128)(2,1)S(1)} %collective-permute-done.13), channel_id=1, source_target_pairs={{0,15},{1,0},{2,1},{3,2},{4,3},{5,4},{6,5},{7,6},{8,7},{9,8},{10,9... | collective-permute-start | bytes 49160 | tf_op jit(solution)/shard_map/ppermute | solution.py:18
  70.6 70.1 %copy-start.1 = (bf16[512,512]{1,0:T(8,128)(2,1)S(1)}, bf16[512,512]{1,0:T(8,128)(2,1)}, u32[]{:S(2)}) copy-start(bf16[512,512]{1,0:T(8,128)(2,1)} %param.19) | copy-start | bytes 1572868
  70.6 70.0 %copy-start.2 = (bf16[512,512]{1,0:T(8,128)(2,1)S(1)}, bf16[512,512]{1,0:T(8,128)(2,1)}, u32[]{:S(2)}) copy-start(bf16[512,512]{1,0:T(8,128)(2,1)} %param.18) | copy-start | bytes 1572868
  70.6 70.0 %copy-start.3 = (bf16[16,512]{1,0:T(8,128)(2,1)S(1)}, bf16[16,512]{1,0:T(8,128)(2,1)}, u32[]{:S(2)}) copy-start(bf16[16,512]{1,0:T(8,128)(2,1)} %param.10) | copy-start | bytes 49156
Sparse Core Ops, SparseCore 0:
  81.0 57.7 reduce-scatter.1
